TPU v7x, 1024 devices: a whole 8x8x8 slice. The times are simulated.
1024 devices in a mesh: lb: 16 (over x, core), rb: 8 (over z), rep: 8 (over y).
Axes of the slice: x: 8, y: 8, z: 8, core: 2. Of those that a mesh axis runs over, the one named last changes fastest.
Arguments:
- left_factor: bfloat16 [1024, 1024], P('lb', 'rep'), may hold values from -5 to 5
- boundary_site: bfloat16 [1024, 16, 1024], P('rep', None, 'rb'), may hold values from -6 to 6
- double_layer: float32 [16, 16], replicated, may hold values from -1.5 to 1.5
Outputs:
- site_q: float32 [16, 1024, 1024], P('rep', 'lb', 'rb')
- factor: float32 [1024, 1024], P('lb')
All inputs are finite; a program needn't handle non-finite values.
Results may differ from a plain program's by a relative error of at most 0.0032.
Values sent between devices are 32-bit elements; how exact they have to be, the bound alone decides.
A program may use at most 64 MiB of HBM per device.

v0:
```python
import math

import jax
import jax.numpy as jnp
from jax import lax
from jax.sharding import PartitionSpec as P

CHI = 1024
PHYS = 16


def shards(left_factor, boundary_site, double_layer):
    highest = lax.Precision.HIGHEST
    absorbed = jnp.einsum(
        "kur,ue->ker", boundary_site.astype(jnp.float32), double_layer, precision=highest
    ).astype(jnp.bfloat16)
    row_count = left_factor.shape[0]
    grown_part = lax.psum_scatter(
        jnp.einsum("ik,ker->eir", left_factor, absorbed, preferred_element_type=jnp.float32),
        "rep",
        scatter_dimension=0,
        tiled=True,
    )
    grown_all = lax.all_gather(grown_part, "lb", axis=1, tiled=True)
    gram_part = jnp.einsum("eir,ejr->ij", grown_part, grown_all, precision=highest)
    gram_block = lax.psum(gram_part, ("rb", "rep"))
    gram = lax.all_gather(gram_block, "lb", axis=0, tiled=True)
    lower = jnp.linalg.cholesky(gram)
    east_count = grown_all.shape[0]
    right_count = grown_all.shape[2]
    matrix = jnp.transpose(grown_all, (1, 0, 2)).reshape(CHI, east_count * right_count)
    solved = jax.scipy.linalg.solve_triangular(lower, matrix, lower=True)
    offset = lax.axis_index("lb") * row_count
    mine = lax.dynamic_slice_in_dim(solved, offset, row_count, 0)
    scale = math.sqrt(PHYS * CHI)
    site_q = jnp.transpose(mine.reshape(row_count, east_count, right_count), (1, 0, 2)) * scale
    factor = lax.dynamic_slice_in_dim(lower, offset, row_count, 0) / scale
    return (site_q, factor)


def solution(mesh):
    return jax.shard_map(
        shards,
        mesh=mesh,
        in_specs=(P("lb", "rep"), P("rep", None, "rb"), P()),
        out_specs=(P("rep", "lb", "rb"), P("lb", None)),
        check_vma=False,
    )
```

profile of v0, /device:TPU:1, one launch (start us, length us, event | category | flops | bytes accessed | tf_op | source)
XLA Modules:
  0.0 674.2 jit_solution(7649725855206367631)
XLA Ops:
  11.3 49.9 %reduce-scatter.2.cloned.1.call-done = f32[2,64,128]{2,1,0:T(8,128)} async-done(((f32[16,64,128]{2,1,0:T(8,128)}), f32[2,64,128]{2,1,0:T(8,128)}) %reduce-scatter.2.cloned.1.call-update) | async-done | bytes 65552 | tf_op jit(solution)/shard_map/reduce_scatter | solution.py:18
  61.3 51.0 %all-gather.3.cloned.1.call-done = f32[2,1024,128]{2,1,0:T(8,128)} async-done(((f32[2,64,128]{2,1,0:T(8,128)}), f32[2,1024,128]{2,1,0:T(8,128)}) %all-gather.3.cloned.1.call-update) | async-done | bytes 1048592 | tf_op jit(solution)/shard_map/all_gather | solution.py:24
  112.3 3.1 convolution_bitcast_fusion.1
  115.5 163.9 %all-reduce.3.cloned.1.call-done = f32[64,1024]{1,0:T(8,128)} async-done(((f32[64,1024]{1,0:T(8,128)}), f32[64,1024]{1,0:T(8,128)}) %all-reduce.3.cloned.1.call-update) | async-done | bytes 262160 | tf_op jit(solution)/shard_map/psum | solution.py:26
  282.4 47.2 %all-gather.5.cloned.1.call-done = f32[1024,1024]{1,0:T(8,128)} async-done(((f32[64,1024]{1,0:T(8,128)}), f32[1024,1024]{1,0:T(8,128)}) %all-gather.5.cloned.1.call-update) | async-done | bytes 4194320 | tf_op jit(solution)/shard_map/all_gather | solution.py:27
  329.5 5.6 copy.21
  335.2 4.4 fusion
  341.5 11.7 %cholesky.223 = f32[128,128]{1,0:T(8,128)S(1)} custom-call(f32[128,128]{1,0:T(8,128)S(1)} %cholesky.580), custom_call_target="Cholesky" | custom-call | tf_op jit(solution)/shard_map/jit(cholesky)/cholesky | solution.py:28
  353.3 9.8 %custom-call.63 = f32[1,128,128]{1,2,0:T(8,128)S(1)} custom-call(f32[1,128,128]{2,1,0:T(8,128)S(1)} %get-tuple-element.76), custom_call_target="InvertDiagBlocksLowerTriangular" | custom-call | tf_op jit(solution)/shard_map/jit(cholesky)/cholesky | solution.py:28
  363.1 2.5 cholesky.255
  365.6 2.3 constant_dynamic-update-slice_fusion.31
  369.5 12.2 %cholesky.244 = f32[128,128]{1,0:T(8,128)S(1)} custom-call(f32[128,128]{1,0:T(8,128)S(1)} %cholesky.584), custom_call_target="Cholesky" | custom-call | tf_op jit(solution)/shard_map/jit(cholesky)/cholesky | solution.py:28
  382.4 9.8 %custom-call.64 = f32[1,128,128]{1,2,0:T(8,128)S(1)} custom-call(f32[1,128,128]{2,1,0:T(8,128)S(1)} %get-tuple-element.73), custom_call_target="InvertDiagBlocksLowerTriangular" | custom-call | tf_op jit(solution)/shard_map/jit(cholesky)/cholesky | solution.py:28
  395.5 11.7 %cholesky.468 = f32[128,128]{1,0:T(8,128)S(1)} custom-call(f32[128,128]{1,0:T(8,128)S(1)} %cholesky.589), custom_call_target="Cholesky" | custom-call | tf_op jit(solution)/shard_map/jit(cholesky)/cholesky | solution.py:28
  408.5 9.8 %custom-call.65 = f32[1,128,128]{1,2,0:T(8,128)S(1)} custom-call(f32[1,128,128]{2,1,0:T(8,128)S(1)} %get-tuple-element.70), custom_call_target="InvertDiagBlocksLowerTriangular" | custom-call | tf_op jit(solution)/shard_map/jit(cholesky)/cholesky | solution.py:28
  419.5 2.3 convolution_subtract_fusion.2
  421.9 11.8 %cholesky.487 = f32[128,128]{1,0:T(8,128)S(1)} custom-call(f32[128,128]{1,0:T(8,128)S(1)} %cholesky.594), custom_call_target="Cholesky" | custom-call | tf_op jit(solution)/shard_map/jit(cholesky)/cholesky | solution.py:28
  435.0 9.8 %custom-call.66 = f32[1,128,128]{1,2,0:T(8,128)S(1)} custom-call(f32[1,128,128]{2,1,0:T(8,128)S(1)} %get-tuple-element.67), custom_call_target="InvertDiagBlocksLowerTriangular" | custom-call | tf_op jit(solution)/shard_map/jit(cholesky)/cholesky | solution.py:28
  446.0 2.3 convolution_subtract_fusion.3
  448.3 11.7 %cholesky.506 = f32[128,128]{1,0:T(8,128)S(1)} custom-call(f32[128,128]{1,0:T(8,128)S(1)} %cholesky.599), custom_call_target="Cholesky" | custom-call | tf_op jit(solution)/shard_map/jit(cholesky)/cholesky | solution.py:28
  461.4 10.0 %custom-call.67 = f32[1,128,128]{1,2,0:T(8,128)S(1)} custom-call(f32[1,128,128]{2,1,0:T(8,128)S(1)} %get-tuple-element.64), custom_call_target="InvertDiagBlocksLowerTriangular" | custom-call | tf_op jit(solution)/shard_map/jit(cholesky)/cholesky | solution.py:28
  472.4 2.3 convolution_subtract_fusion.4
  474.7 11.7 %cholesky.526 = f32[128,128]{1,0:T(8,128)S(1)} custom-call(f32[128,128]{1,0:T(8,128)S(1)} %cholesky.604), custom_call_target="Cholesky" | custom-call | tf_op jit(solution)/shard_map/jit(cholesky)/cholesky | solution.py:28
  487.7 9.8 %custom-call.68 = f32[1,128,128]{1,2,0:T(8,128)S(1)} custom-call(f32[1,128,128]{2,1,0:T(8,128)S(1)} %get-tuple-element.61), custom_call_target="InvertDiagBlocksLowerTriangular" | custom-call | tf_op jit(solution)/shard_map/jit(cholesky)/cholesky | solution.py:28
  500.5 12.1 %cholesky.546 = f32[128,128]{1,0:T(8,128)S(1)} custom-call(f32[128,128]{1,0:T(8,128)S(1)} %cholesky.609), custom_call_target="Cholesky" | custom-call | tf_op jit(solution)/shard_map/jit(cholesky)/cholesky | solution.py:28
  513.9 9.8 %custom-call.69 = f32[1,128,128]{1,2,0:T(8,128)S(1)} custom-call(f32[1,128,128]{2,1,0:T(8,128)S(1)} %get-tuple-element.58), custom_call_target="InvertDiagBlocksLowerTriangular" | custom-call | tf_op jit(solution)/shard_map/jit(cholesky)/cholesky | solution.py:28
  526.3 11.7 %cholesky.564 = f32[128,128]{1,0:T(8,128)S(1)} custom-call(f32[128,128]{1,0:T(8,128)S(1)} %convolution_subtract_fusion.13), custom_call_target="Cholesky" | custom-call | tf_op jit(solution)/shard_map/jit(cholesky)/cholesky | solution.py:28
  545.0 6.6 fusion.1
  551.6 22.6 %while.1 = (s32[]{:T(128)}, f32[1024,1024]{1,0:T(8,128)}, s32[8,2]{0,1:T(2,128)S(1)}, f32[8,128,128]{2,1,0:T(8,128)S(1)}, s32[]{:T(128)}) while((s32[]{:T(128)}, f32[1024,1024]{1,0:T(8,128)}, s32[8,2]{0,1:T(2,128)S(1)}, f32[8,128,128]{2,1,0:T(8,128)S(1)}, s32[]{:T(128)}) %tuple.69), condition=%wide.while_cond, body=%wide.while_body.sunk | while | flops 2 | bytes 131189 | solution.py:32
  552.2 2.2 bitcast_dynamic-update-slice_fusion.2
  555.0 2.2 bitcast_dynamic-update-slice_fusion.2
  574.2 78.8 %custom-call.70 = f32[8,128,128]{1,2,0:T(8,128)S(1)} custom-call(f32[8,128,128]{2,1,0:T(8,128)S(1)} %get-tuple-element.9), custom_call_target="InvertDiagBlocksLowerTriangular" | custom-call | tf_op jit(solution)/shard_map/jit(_solve_triangular)/triangular_solve | solution.py:32
  (104 shorter events, 64.4 us)
Async XLA Ops:
  7.2 1.0 copy-start
  7.2 54.0 %reduce-scatter.2.cloned.1.call-start = ((), (), s32[]{:S(2)}) async-start(), calls=%async_computation.1 | async-start | bytes 589824 | tf_op jit(solution)/shard_map/reduce_scatter | solution.py:18
  11.3 101.0 %all-gather.3.cloned.1.call-start = ((), (), s32[]{:S(2)}) async-start(), calls=%async_computation.2 | async-start | bytes 1114112 | tf_op jit(solution)/shard_map/all_gather | solution.py:24
  61.2 218.2 %all-reduce.3.cloned.1.call-start = ((), (), s32[]{:S(2)}) async-start(), calls=%async_computation.3 | async-start | bytes 524288 | tf_op jit(solution)/shard_map/psum | solution.py:26
  115.4 214.1 %all-gather.5.cloned.1.call-start = ((), (), s32[]{:S(2)}) async-start(), calls=%async_computation.4 | async-start | bytes 4456448 | tf_op jit(solution)/shard_map/all_gather | solution.py:27
  339.6 1.9 copy-start.1
Sparse Core Ops, SparseCore 0:
  11.4 49.7 reduce-scatter.1
  63.9 48.3 all-gather.2
  116.1 163.2 all-reduce.2
  282.0 47.5 all-gather.4
where the time goes:
time: 678 us; the launch traced here: 674 us
  waiting for transfers between devices  312 us (46%)
  other arithmetic  265 us (39%)
  matrix products  41.3 us (6%)
  local copies, waits for them, and re-layouts  36.3 us (5%)
  between operations  19.4 us (3%)
    another operation x30, other arithmetic, shards(): lower = jnp.linalg.cholesky(gram)  173 us
    psum x1, waiting for transfers between devices, shards(): gram_block = lax.psum(gram_part, ('rb', 'rep'))  164 us
    another operation x3, other arithmetic, shards(): solved = jax.scipy.linalg.solve_triangular(lower, matrix, lower=True)  85.3 us
    all_gather x1, waiting for transfers between devices, shards(): grown_all = lax.all_gather(grown_part, 'lb', axis=1, tiled=True)  51 us
    reduce_scatter x1, waiting for transfers between devices, shards(): lax.psum_scatter(jnp.einsum('ik,ker->eir', left_factor, absorbed, preferr...  49.9 us
    all_gather x1, waiting for transfers between devices, shards(): gram = lax.all_gather(gram_block, 'lb', axis=0, tiled=True)  47.2 us
    another operation x14, matrix products, shards(): lower = jnp.linalg.cholesky(gram)  23 us
    another operation x24, local copies, waits for them, and re-layouts  22.4 us
  transfers between devices with their start and end apart: 4, of which 4 were waited for; matrix products, arithmetic and copies ran while one was open for 0% of the time, Pallas kernels for 0%

commit v1 on v0

v1 whole, which is shorter than its diff:
```python
import jax
import jax.numpy as jnp
from jax import lax
from jax.experimental import pallas as pl
from jax.experimental.pallas import tpu as pltpu
from jax.sharding import PartitionSpec as P

CHI = 1024
BLOCK = 128
TILES = BLOCK // 8
F32 = jnp.float32
BF16 = jnp.bfloat16


NT = (((1,), (1,)), ((), ()))
NN = (((1,), (0,)), ((), ()))


def dot(a, b, dims):
    return lax.dot_general(a, b, dims, precision=lax.Precision.HIGHEST, preferred_element_type=F32)


def factor_block(r_ref):
    sub = lax.broadcasted_iota(jnp.int32, (8, BLOCK), 0)

    def spread(tile, row):
        return jnp.broadcast_to(tile[row : row + 1, :], (8, BLOCK))

    for t in range(TILES):
        at = pl.ds(8 * t, 8)
        left, right = r_ref[at, :BLOCK], r_ref[at, BLOCK:]
        cols = [jnp.broadcast_to(left[:, 8 * t + n : 8 * t + n + 1], (8, BLOCK)) for n in range(8)]
        roots, lefts, rights, links = [], [], [], []
        scale = jnp.zeros((8, BLOCK), F32)
        for i in range(8):
            root = lax.rsqrt(spread(cols[i], i))
            scale = jnp.where(sub == i, root, scale)
            below = jnp.where(sub > i, cols[i] * root, 0.0)
            ul, ur = spread(left, i) * root, spread(right, i) * root
            link = {n: spread(cols[n], i) * root for n in range(i + 1, 8)}
            for n in range(i + 1, 8):
                cols[n] = cols[n] - below * link[n]
            left, right = left - below * ul, right - below * ur
            roots.append(root)
            lefts.append(ul)
            rights.append(ur)
            links.append(link)
        r_ref[at, :BLOCK] = left * scale
        r_ref[at, BLOCK:] = right * scale
        for s in range(t + 1, TILES):
            low = pl.ds(8 * s, 8)
            left, right = r_ref[low, :BLOCK], r_ref[low, BLOCK:]
            cols = [jnp.broadcast_to(left[:, 8 * t + n : 8 * t + n + 1], (8, BLOCK)) for n in range(8)]
            for i in range(8):
                below = cols[i] * roots[i]
                for n in range(i + 1, 8):
                    cols[n] = cols[n] - below * links[i][n]
                left, right = left - below * lefts[i], right - below * rights[i]
            r_ref[low, :BLOCK] = left
            r_ref[low, BLOCK:] = right


def factor_kernel(lb_fn, a_ref, g_ref, q_ref, f_ref, r_ref):
    blocks = CHI // BLOCK
    row = lax.broadcasted_iota(jnp.int32, (BLOCK, BLOCK), 0)
    col = lax.broadcasted_iota(jnp.int32, (BLOCK, BLOCK), 1)

    def body(j, carry):
        here = pl.ds(pl.multiple_of(j * BLOCK, BLOCK), BLOCK)
        r_ref[:, :BLOCK] = a_ref[here, here]
        r_ref[:, BLOCK:] = jnp.where(row == col, 1.0, 0.0).astype(F32)
        factor_block(r_ref)
        for jj in range(blocks):
            @pl.when(j == jj)
            def _():
                lo, hi = jj * BLOCK, (jj + 1) * BLOCK
                inv = jnp.where(row >= col, r_ref[:, BLOCK:], 0.0)
                d = dot(a_ref[lo:hi, lo:hi], inv, NT)
                a_ref[lo:hi, lo:hi] = jnp.where(row >= col, d, 0.0)
                y = []
                for h in range(2):
                    yh = dot(inv, g_ref[h, lo:hi, :], NN)
                    g_ref[h, lo:hi, :] = yh
                    y.append(yh)
                if hi < CHI:
                    a_ref[hi:, lo:hi] = dot(a_ref[hi:, lo:hi], inv, NT)
                for i in range(jj + 1, blocks):
                    mine = pl.ds(i * BLOCK, BLOCK)
                    p = a_ref[mine, lo:hi]
                    a_ref[mine, hi : (i + 1) * BLOCK] -= dot(p, a_ref[hi : (i + 1) * BLOCK, lo:hi], NT)
                    for h in range(2):
                        g_ref[h, mine, :] -= dot(p, y[h], NN)
        return carry

    lax.fori_loop(0, blocks, body, 0)
    lb = lb_fn()
    at = pl.ds(pl.multiple_of(lb * 64, 64), 64)
    for h in range(2):
        q_ref[h] = g_ref[h, at, :] * 128.0
    rr = lb * 64 + lax.broadcasted_iota(jnp.int32, (64, CHI), 0)
    cc = lax.broadcasted_iota(jnp.int32, (64, CHI), 1)
    f_ref[...] = jnp.where(rr >= cc, a_ref[at, :], 0.0) * (1.0 / 128.0)


def factor_call(gram, grown, lb_fn):
    def kernel(a_in, g_in, q_ref, f_ref, a_ref, g_ref, r_ref):
        a_ref[...] = a_in[...]
        g_ref[...] = g_in[...]
        factor_kernel(lb_fn, a_ref, g_ref, q_ref, f_ref, r_ref)

    vm = pl.BlockSpec(memory_space=pltpu.VMEM)
    return pl.pallas_call(
        kernel,
        out_shape=(jax.ShapeDtypeStruct((2, 64, 128), F32), jax.ShapeDtypeStruct((64, CHI), F32)),
        in_specs=[vm, vm],
        out_specs=(vm, vm),
        scratch_shapes=[pltpu.VMEM((CHI, CHI), F32), pltpu.VMEM((2, CHI, 128), F32), pltpu.VMEM((BLOCK, 2 * BLOCK), F32)],
        compiler_params=pltpu.CompilerParams(vmem_limit_bytes=40 << 20),
    )(gram, grown)


def shards(left_factor, boundary_site, double_layer):
    highest = lax.Precision.HIGHEST
    absorbed = jnp.einsum(
        "kur,ue->ker", boundary_site.astype(F32), double_layer, precision=highest
    ).astype(BF16)
    grown_part = lax.psum_scatter(
        jnp.einsum("ik,ker->eir", left_factor, absorbed, preferred_element_type=F32),
        "rep",
        scatter_dimension=0,
        tiled=True,
    )
    grown_all = lax.all_gather(grown_part, "lb", axis=1, tiled=True)
    gram_part = jnp.einsum("eir,ejr->ij", grown_part, grown_all, precision=highest)
    tiles = gram_part.reshape(8, 8, 8, 128).transpose(0, 2, 1, 3).reshape(512, 128)
    tile = lax.psum_scatter(tiles, "rb", scatter_dimension=0, tiled=True)
    tile = lax.psum_scatter(tile, "rep", scatter_dimension=0, tiled=True)
    tiles = lax.all_gather(tile, ("lb", "rb", "rep"), axis=0, tiled=True)
    gram = tiles.reshape(128, 8, 8, 128).transpose(0, 2, 1, 3).reshape(CHI, CHI)
    return factor_call(gram, grown_all, lambda: lax.axis_index("lb"))


def solution(mesh):
    return jax.shard_map(
        shards,
        mesh=mesh,
        in_specs=(P("lb", "rep"), P("rep", None, "rb"), P()),
        out_specs=(P("rep", "lb", "rb"), P("lb", None)),
        check_vma=False,
    )
```

time: 678 us -> 377 us (0.56)
  other arithmetic: 265 us -> 0 us
  Pallas kernels: 0 us -> 48.9 us
  matrix products: 41.3 us -> 6.13 us
  waiting for transfers between devices: 312 us -> 277 us
  local copies, waits for them, and re-layouts: 36.3 us -> 6.27 us
  blocking collectives: 0 us -> 23.6 us
    another operation x33 -> x0, other arithmetic: 258 us -> none  [the longest x30 173 us: shards(): lower = jnp.linalg.cholesky(gram)]
    psum x1 -> x0, waiting for transfers between devices: 164 us -> none  [shards(): gram_block = lax.psum(gram_part, ('rb', 'rep'))]
    all_gather x1, waiting for transfers between devices: 47.2 us -> 139 us  [shards(): tiles = lax.all_gather(tile, ('lb', 'rb', 'rep'), axis=0, tiled=True)]
    pallas_call x0 -> x1, Pallas kernels: none -> 48.9 us  [factor_call(): pl.pallas_call(kernel, out_shape=(jax.ShapeDtypeStruct((2, 64, 128), F32)...]
    reduce_scatter x0 -> x1, waiting for transfers between devices: none -> 37.3 us  [shards(): tile = lax.psum_scatter(tiles, 'rb', scatter_dimension=0, tiled=True)]
    another operation x29 -> x0, matrix products: 35.1 us -> none  [the longest x14 23 us: shards(): lower = jnp.linalg.cholesky(gram)]
    another operation x49 -> x0, local copies, waits for them, and re-layouts: 27.8 us -> none
    unnamed x0 -> x1, blocking collectives: none -> 23.6 us
where the time goes in v1:
time: 377 us; the launch traced here: 376 us
  waiting for transfers between devices  277 us (73%)
  Pallas kernels  48.9 us (13%)
  blocking collectives  23.6 us (6%)
  between operations  14.4 us (4%)
  local copies, waits for them, and re-layouts  6.27 us (2%)
  matrix products  6.13 us (2%)
    all_gather x1, waiting for transfers between devices, shards(): tiles = lax.all_gather(tile, ('lb', 'rb', 'rep'), axis=0, tiled=True)  139 us
    all_gather x1, waiting for transfers between devices, shards(): grown_all = lax.all_gather(grown_part, 'lb', axis=1, tiled=True)  51 us
    reduce_scatter x1, waiting for transfers between devices, shards(): lax.psum_scatter(jnp.einsum('ik,ker->eir', left_factor, absorbed, preferr...  49.9 us
    pallas_call x1, Pallas kernels, factor_call(): pl.pallas_call(kernel, out_shape=(jax.ShapeDtypeStruct((2, 64, 128), F32)...  48.9 us
    reduce_scatter x1, waiting for transfers between devices, shards(): tile = lax.psum_scatter(tiles, 'rb', scatter_dimension=0, tiled=True)  37.3 us
    unnamed x1, blocking collectives  23.6 us
  transfers between devices with their start and end apart: 4, of which 4 were waited for; matrix products, arithmetic and copies ran while one was open for 0% of the time, Pallas kernels for 0%

profile of v1, /device:TPU:1, one launch (start us, length us, event | category | flops | bytes accessed | tf_op | source)
XLA Modules:
  0.0 376.5 jit_solution(13550595402836765671)
XLA Ops:
  7.2 0.0 copy-start
  7.2 0.0 reduce-scatter.3.cloned.1.call-start
  7.2 1.0 copy-done
  8.2 1.3 fusion.3
  9.5 1.7 convolution_bitcast_fusion
  11.3 0.0 reduce-scatter.3.cloned.1.call-update
  11.3 0.0 all-gather.3.cloned.1.call-start
  11.3 49.9 %reduce-scatter.3.cloned.1.call-done = f32[2,64,128]{2,1,0:T(8,128)} async-done(((f32[16,64,128]{2,1,0:T(8,128)}), f32[2,64,128]{2,1,0:T(8,128)}) %reduce-scatter.3.cloned.1.call-update) | async-done | bytes 65552 | tf_op jit(solution)/shard_map/reduce_scatter | solution.py:127
  61.2 0.0 all-gather.3.cloned.1.call-update
  61.2 0.0 reduce-scatter.5.cloned.1.call-start
  61.3 51.0 %all-gather.3.cloned.1.call-done.g_in = f32[2,1024,128]{2,1,0:T(8,128)} async-done(((f32[2,64,128]{2,1,0:T(8,128)}), f32[2,1024,128]{2,1,0:T(8,128)}) %all-gather.3.cloned.1.call-update) | async-done | bytes 1048592 | tf_op jit(solution)/shard_map/all_gather | solution.py:133
  112.3 3.1 fusion.5
  115.4 0.0 reduce-scatter.5.cloned.1.call-update
  115.4 0.0 all-gather.5.cloned.1.call-start
  115.5 1.3 dynamic-slice
  117.4 37.3 %reduce-scatter.5.cloned.1.call-done = f32[64,128]{1,0:T(8,128)} async-done(((f32[512,128]{1,0:T(8,128)}), f32[64,128]{1,0:T(8,128)}) %reduce-scatter.5.cloned.1.call-update) | async-done | bytes 32784 | tf_op jit(solution)/shard_map/reduce_scatter | solution.py:136
  154.8 23.6 %all-reduce = f32[64,128]{1,0:T(8,128)S(1)} all-reduce(f32[64,128]{1,0:T(8,128)} %reduce-scatter.5.cloned.1.call-done), channel_id=4, replica_groups=mesh['lb'=16,'rb'=8,'rep'=8] {'rep'}, use_global_device_ids=true, to_apply=%region_2.0.clone | all-reduce | flops 8192 | bytes 65536
  178.4 0.6 constant_dynamic-slice_fusion
  178.9 0.0 all-gather.5.cloned.1.call-update
  179.0 138.6 %all-gather.5.cloned.1.call-done = f32[8192,128]{1,0:T(8,128)} async-done(((f32[8,128]{1,0:T(8,128)}), f32[8192,128]{1,0:T(8,128)}) %all-gather.5.cloned.1.call-update) | async-done | bytes 4194320 | tf_op jit(solution)/shard_map/all_gather | solution.py:138
  317.6 0.0 copy-start.1
  317.6 2.2 copy-done.1
  319.8 0.0 copy-start.2
  319.8 1.2 copy-done.2
  321.0 48.9 %shard_map.50 = (f32[2,64,128]{2,1,0:T(8,128)}, f32[64,1024]{1,0:T(8,128)}) custom-call(f32[1024,1024]{1,0:T(8,128)S(1)} %bitcast.27, f32[2,1024,128]{2,1,0:T(8,128)S(1)} %copy-done.2), custom_call_target="tpu_custom_call" | custom-call | tf_op jit(solution)/shard_map/pallas_call | solution.py:112
Async XLA Ops:
  7.2 1.0 copy-start
  7.2 54.0 %reduce-scatter.3.cloned.1.call-start = ((), (), s32[]{:S(2)}) async-start(), calls=%async_computation.2 | async-start | bytes 589824 | tf_op jit(solution)/shard_map/reduce_scatter | solution.py:127
  11.3 101.0 %all-gather.3.cloned.1.call-start = ((), (), s32[]{:S(2)}) async-start(), calls=%async_computation.3 | async-start | bytes 1114112 | tf_op jit(solution)/shard_map/all_gather | solution.py:133
  61.2 93.5 %reduce-scatter.5.cloned.1.call-start = ((), (), s32[]{:S(2)}) async-start(), calls=%async_computation.4 | async-start | bytes 294912 | tf_op jit(solution)/shard_map/reduce_scatter | solution.py:136
  115.4 202.2 %all-gather.5.cloned.1.call-start = ((), (), s32[]{:S(2)}) async-start(), calls=%async_computation.5 | async-start | bytes 4198400 | tf_op jit(solution)/shard_map/all_gather | solution.py:138
  317.6 2.2 copy-start.1
  319.8 1.2 copy-start.2
Sparse Core Ops, SparseCore 0:
  11.4 49.7 reduce-scatter.2
  63.9 48.3 all-gather.2
  116.3 38.4 reduce-scatter.4
  179.1 138.4 all-gather.4

commit v2 on v1

--- a/solution.py
+++ b/solution.py
@@ -102,9 +102,252 @@
     f_ref[...] = jnp.where(rr >= cc, a_ref[at, :], 0.0) * (1.0 / 128.0)
 
 
+MESH = pl.DeviceIdType.MESH
+
+
+def mod(value, size):
+    return lax.rem(value + 2 * size, size)
+
+
+def gather_kernel(sizes, part_ref, grown_ref, gram_ref, a_recv, products, z_recv, total, y_recv, tile, sems):
+    nx, nz, ny = sizes
+    lb, z, y = lax.axis_index("lb"), lax.axis_index("rb"), lax.axis_index("rep")
+    x, core = lb // 2, lax.rem(lb, 2)
+    half = nx // 2
+    (a_send, a_got, b_send, b_got, p_send, p_got, c_send, c_got, d_send, d_got,
+     e_send, e_got, f_send, f_got, g_send, g_got, h_send, h_got) = sems
+
+    def remote(src, dst, send, got, target):
+        return pltpu.make_async_remote_copy(
+            src_ref=src, dst_ref=dst, send_sem=send, recv_sem=got, device_id=target, device_id_type=MESH
+        )
+
+    barrier = pltpu.get_barrier_semaphore()
+    for d in range(1, ny):
+        pl.semaphore_signal(barrier, inc=1, device_id={"rep": mod(y + d, ny)}, device_id_type=MESH)
+    for d in range(1, nz):
+        pl.semaphore_signal(barrier, inc=1, device_id={"rb": mod(z + d, nz)}, device_id_type=MESH)
+    for d in range(1, 2 * nx):
+        pl.semaphore_signal(barrier, inc=1, device_id={"lb": mod(lb + d, 2 * nx)}, device_id_type=MESH)
+    pl.semaphore_wait(barrier, ny - 1 + nz - 1 + 2 * nx - 1)
+
+    def far_first(n):
+        return sorted(range(1, n), key=lambda d: -min(d, n - d))
+
+    copies = []
+    for d in far_first(ny):
+        to = mod(y + d, ny)
+        copy = remote(part_ref.at[pl.ds(2 * to, 2)], a_recv.at[d - 1], a_send.at[d - 1], a_got.at[d - 1], {"rep": to})
+        copy.start()
+        copies.append(copy)
+    mine = part_ref[pl.ds(2 * y, 2)]
+    for copy, d in sorted(zip(copies, far_first(ny)), key=lambda pair: min(pair[1], ny - pair[1])):
+        copy.wait_recv()
+        mine = mine + a_recv[d - 1]
+    rows = pl.ds(pl.multiple_of(lb * 64, 64), 64)
+    for e in range(2):
+        grown_ref[e, rows, :] = mine[e]
+    sent = list(copies)
+
+    def block(e, chip, which):
+        return grown_ref.at[e, pl.ds(pl.multiple_of((2 * chip + which) * 64, 64), 64)]
+
+    partner = {"lb": 2 * x + 1 - core}
+    handed = []
+
+    def hand(e, chip, slot):
+        copy = remote(block(e, chip, core), block(e, chip, core), p_send.at[slot], p_got.at[slot], partner)
+        copy.start()
+        handed.append(copy)
+
+    def ring(direction, step, e):
+        chip = mod(x - direction * (step - 1), nx)
+        side = 0 if direction > 0 else 1
+        slot = (side * half + step - 1) * 2 + e
+        to = {"lb": 2 * mod(x + direction, nx) + core}
+        copy = remote(block(e, chip, core), block(e, chip, core), b_send.at[slot], b_got.at[slot], to)
+        copy.start()
+        sent.append(copy)
+        return copy
+
+    def moves(step):
+        full = [(direction, e) for e in range(2) for direction in (1, -1)]
+        return full if step < half else [(1, 0), (-1, 1)]
+
+    flying = {}
+    for direction, e in moves(1):
+        flying[direction, 1, e] = ring(direction, 1, e)
+    for e in range(2):
+        hand(e, x, e)
+    slot = 2
+    for step in range(1, half + 1):
+        for direction, e in moves(step):
+            flying[direction, step, e].wait_recv()
+            if step < half and (direction, e) in moves(step + 1):
+                flying[direction, step + 1, e] = ring(direction, step + 1, e)
+            hand(e, mod(x - direction * step, nx), slot)
+            slot += 1
+    for copy in handed:
+        copy.wait_recv()
+    sent += handed
+
+    ours = [grown_ref[e, rows, :] for e in range(2)]
+    copies = []
+    for d in far_first(nz) + [0]:
+        to = mod(z + d, nz)
+        at = pl.ds(pl.multiple_of(to * 128, 128), 128)
+        products[d] = dot(ours[0], grown_ref[0, at, :], NT) + dot(ours[1], grown_ref[1, at, :], NT)
+        if d:
+            copy = remote(products.at[d], z_recv.at[d - 1], c_send.at[d - 1], c_got.at[d - 1], {"rb": to})
+            copy.start()
+            copies.append((d, copy))
+    summed = products[0]
+    for d, copy in sorted(copies, key=lambda pair: min(pair[0], nz - pair[0])):
+        copy.wait_recv()
+        summed = summed + z_recv[d - 1]
+    total[...] = summed
+    sent += [copy for _, copy in copies]
+    copies = []
+    for d in far_first(ny):
+        to = mod(y + d, ny)
+        src = total.at[pl.ds(pl.multiple_of(8 * to, 8), 8)]
+        copy = remote(src, y_recv.at[d - 1], d_send.at[d - 1], d_got.at[d - 1], {"rep": to})
+        copy.start()
+        copies.append((d, copy))
+    summed = total[pl.ds(pl.multiple_of(8 * y, 8), 8), :]
+    for d, copy in sorted(copies, key=lambda pair: min(pair[0], ny - pair[0])):
+        copy.wait_recv()
+        summed = summed + y_recv[d - 1]
+    tile[...] = summed
+    sent += [copy for _, copy in copies]
+
+    def place(which):
+        return z * (1 - which) + y * which, y * (1 - which) + z * which
+
+    side = lb // nx
+    outer, inner = place(side)
+    spot = lax.rem(lb, nx)
+    home = gram_ref.at[side, outer, inner, pl.ds(pl.multiple_of(8 * spot, 8), 8)]
+    copies = []
+    for d in far_first(nx):
+        copy = remote(tile, home, e_send.at[d], e_got.at[spot], {"lb": 2 * mod(x + d, nx) + side})
+        copy.start()
+        copies.append(copy)
+    across = remote(tile, home, e_send.at[0], e_got.at[spot], partner)
+    here = pltpu.make_async_copy(tile, home, e_got.at[spot])
+
+    @pl.when(core == side)
+    def _():
+        here.start()
+
+    @pl.when(core != side)
+    def _():
+        across.start()
+        across.wait_send()
+
+    sent += copies
+    outer, inner = place(core)
+    for i in range(nx):
+        landed = gram_ref.at[core, outer, inner, pl.ds(8 * i, 8)]
+        pltpu.make_async_copy(tile, landed, e_got.at[i]).wait()
+
+    n = ny
+    copies = []
+    chunk = gram_ref.at[core, outer, inner]
+    for d in far_first(n):
+        to = {"rep": mod(y + d * (1 - core), n), "rb": mod(z + d * core, n)}
+        copy = remote(chunk, chunk, f_send.at[d - 1], f_got.at[d - 1], to)
+        copy.start()
+        copies.append(copy)
+    for copy in copies:
+        copy.wait_recv()
+    sent += copies
+
+    cuts = 4
+    width = n // cuts
+    middle = n // 2
+
+    def piece(position, cut):
+        return gram_ref.at[core, position, pl.ds(cut * width, width)]
+
+    def around(direction, step, cut):
+        position = mod(outer - direction * (step - 1), n)
+        slot = ((0 if direction > 0 else 1) * middle + step - 1) * cuts + cut
+        to = {"rb": mod(z + direction * (1 - core), n), "rep": mod(y + direction * core, n)}
+        copy = remote(piece(position, cut), piece(position, cut), g_send.at[slot], g_got.at[slot], to)
+        copy.start()
+        sent.append(copy)
+        return copy
+
+    handed = []
+
+    def share(position, cut, slot):
+        copy = remote(piece(position, cut), piece(position, cut), h_send.at[slot], h_got.at[slot], partner)
+        copy.start()
+        handed.append(copy)
+
+    def turns(step):
+        if step < middle:
+            return [(direction, cut) for cut in range(cuts) for direction in (1, -1)]
+        return [(1 if cut < cuts // 2 else -1, cut) for cut in (0, cuts // 2, 1, cuts // 2 + 1)]
+
+    flying = {}
+    for direction, cut in turns(1):
+        flying[direction, 1, cut] = around(direction, 1, cut)
+    for cut in range(cuts):
+        share(outer, cut, cut)
+    slot = cuts
+    for step in range(1, middle + 1):
+        for direction, cut in turns(step):
+            flying[direction, step, cut].wait_recv()
+            if step < middle and (direction, cut) in turns(step + 1):
+                flying[direction, step + 1, cut] = around(direction, step + 1, cut)
+            share(mod(outer - direction * step, n), cut, slot)
+            slot += 1
+    for copy in handed:
+        copy.wait_recv()
+    for copy in sent + handed:
+        copy.wait_send()
+
+
+def gather_call(part, sizes):
+    nx, nz, ny = sizes
+    vm = pl.BlockSpec(memory_space=pltpu.VMEM)
+    counts = [ny - 1] * 2 + [2 * nx] * 4 + [nz - 1] * 2 + [ny - 1] * 2 + [nx] * 2 + [ny - 1] * 2 + [4 * ny] * 4
+
+    def kernel(part_ref, grown_ref, gram_ref, a_recv, products, z_recv, total, y_recv, tile, *sems):
+        gather_kernel(sizes, part_ref, grown_ref, gram_ref, a_recv, products, z_recv, total, y_recv, tile, sems)
+
+    return pl.pallas_call(
+        kernel,
+        out_shape=(
+            jax.ShapeDtypeStruct((2, 128 * nx, 128), F32),
+            jax.ShapeDtypeStruct((2, ny, ny, 8 * nx, 128), F32),
+        ),
+        in_specs=[vm],
+        out_specs=(vm, vm),
+        scratch_shapes=[
+            pltpu.VMEM((ny - 1, 2, 64, 128), F32),
+            pltpu.VMEM((nz, 64, 128), F32),
+            pltpu.VMEM((nz - 1, 64, 128), F32),
+            pltpu.VMEM((64, 128), F32),
+            pltpu.VMEM((ny - 1, 8, 128), F32),
+            pltpu.VMEM((8, 128), F32),
+        ]
+        + [pltpu.SemaphoreType.DMA((count,)) for count in counts],
+        compiler_params=pltpu.CompilerParams(collective_id=0, has_side_effects=True, vmem_limit_bytes=24 << 20),
+    )(part)
+
+
 def factor_call(gram, grown, lb_fn):
     def kernel(a_in, g_in, q_ref, f_ref, a_ref, g_ref, r_ref):
-        a_ref[...] = a_in[...]
+        for outer in range(8):
+            for inner in range(8):
+                for i in range(8):
+                    at = pl.ds(8 * i, 8)
+                    up, low = 64 * i + 8 * inner, 512 + 64 * i + 8 * outer
+                    a_ref[up : up + 8, 128 * outer : 128 * outer + 128] = a_in[0, outer, inner, at, :]
+                    a_ref[low : low + 8, 128 * inner : 128 * inner + 128] = a_in[1, outer, inner, at, :]
         g_ref[...] = g_in[...]
         factor_kernel(lb_fn, a_ref, g_ref, q_ref, f_ref, r_ref)
 
@@ -115,7 +358,7 @@
         in_specs=[vm, vm],
         out_specs=(vm, vm),
         scratch_shapes=[pltpu.VMEM((CHI, CHI), F32), pltpu.VMEM((2, CHI, 128), F32), pltpu.VMEM((BLOCK, 2 * BLOCK), F32)],
-        compiler_params=pltpu.CompilerParams(vmem_limit_bytes=40 << 20),
+        compiler_params=pltpu.CompilerParams(vmem_limit_bytes=24 << 20),
     )(gram, grown)
 
 
@@ -124,20 +367,9 @@
     absorbed = jnp.einsum(
         "kur,ue->ker", boundary_site.astype(F32), double_layer, precision=highest
     ).astype(BF16)
-    grown_part = lax.psum_scatter(
-        jnp.einsum("ik,ker->eir", left_factor, absorbed, preferred_element_type=F32),
-        "rep",
-        scatter_dimension=0,
-        tiled=True,
-    )
-    grown_all = lax.all_gather(grown_part, "lb", axis=1, tiled=True)
-    gram_part = jnp.einsum("eir,ejr->ij", grown_part, grown_all, precision=highest)
-    tiles = gram_part.reshape(8, 8, 8, 128).transpose(0, 2, 1, 3).reshape(512, 128)
-    tile = lax.psum_scatter(tiles, "rb", scatter_dimension=0, tiled=True)
-    tile = lax.psum_scatter(tile, "rep", scatter_dimension=0, tiled=True)
-    tiles = lax.all_gather(tile, ("lb", "rb", "rep"), axis=0, tiled=True)
-    gram = tiles.reshape(128, 8, 8, 128).transpose(0, 2, 1, 3).reshape(CHI, CHI)
-    return factor_call(gram, grown_all, lambda: lax.axis_index("lb"))
+    part = jnp.einsum("ik,ker->eir", left_factor, absorbed, preferred_element_type=F32)
+    grown, gram = gather_call(part, (8, 8, 8))
+    return factor_call(gram, grown, lambda: lax.axis_index("lb"))
 
 
 def solution(mesh):

time: 377 us -> 147 us (0.39)
  waiting for transfers between devices: 277 us -> 0 us
  Pallas kernels: 48.9 us -> 143 us
  blocking collectives: 23.6 us -> 0 us
  between operations: 14.4 us -> 0.66 us
  local copies, waits for them, and re-layouts: 6.27 us -> 1.04 us
  matrix products: 6.13 us -> 2.25 us
    all_gather x2 -> x0, waiting for transfers between devices: 190 us -> none  [the longest x1 139 us: shards(): tiles = lax.all_gather(tile, ('lb', 'rb', 'rep'), axis=0, tiled=True)]
    pallas_call x0 -> x1, Pallas kernels: none -> 93.7 us  [gather_call(): pl.pallas_call(kernel, out_shape=(jax.ShapeDtypeStruct((2, 128 * nx, 128)...]
    reduce_scatter x2 -> x0, waiting for transfers between devices: 87.2 us -> none  [the longest x1 49.9 us: shards(): lax.psum_scatter(jnp.einsum('ik,ker->eir', left_factor, absorbed, preferr...]
    unnamed x1 -> x0, blocking collectives: 23.6 us -> none
    unnamed x8 -> x2, local copies, waits for them, and re-layouts: 6.27 us -> 1.04 us
  transfers between devices with their start and end apart: 4 -> 0, of which waited for: 4 -> 0; matrix products, arithmetic and copies ran while one was open for 0% -> 0% of each run, Pallas kernels for 0% -> 0%
where the time goes in v2:
time: 147 us
  Pallas kernels  143 us (97%)
  matrix products  2.25 us (2%)
    pallas_call x1, Pallas kernels, gather_call(): pl.pallas_call(kernel, out_shape=(jax.ShapeDtypeStruct((2, 128 * nx, 128)...  93.7 us
    pallas_call x1, Pallas kernels, factor_call(): pl.pallas_call(kernel, out_shape=(jax.ShapeDtypeStruct((2, 64, 128), F32)...  49 us

profile of v2, /device:TPU:1, one launch (start us, length us, event | category | flops | bytes accessed | tf_op | source)
XLA Modules:
  0.0 146.7 jit_solution(8702690528011676263)
XLA Ops:
  0.6 0.0 copy-start
  0.6 1.0 copy-done
  1.7 1.3 fusion.3
  3.0 0.9 convolution_bitcast_fusion.part_ref
  3.9 93.7 %shard_map.50 = (f32[2,1024,128]{2,1,0:T(8,128)S(1)}, f32[2,8,8,64,128]{4,3,2,1,0:T(8,128)S(1)}) custom-call(f32[16,64,128]{2,1,0:T(8,128)S(1)} %convolution_bitcast_fusion.part_ref), custom_call_target="tpu_custom_call" | custom-call | tf_op jit(solution)/shard_map/pallas_call | solution.py:321
  97.7 49.0 %shard_map.51 = (f32[2,64,128]{2,1,0:T(8,128)}, f32[64,1024]{1,0:T(8,128)}) custom-call(f32[2,8,8,64,128]{4,3,2,1,0:T(8,128)S(1)} %get-tuple-element.4.a_in, f32[2,1024,128]{2,1,0:T(8,128)S(1)} %get-tuple-element.5.g_in), custom_call_target="tpu_custom_call" | custom-call | tf_op jit(solution)/shard_map/pallas_call | solution.py:355
Async XLA Ops:
  0.6 1.0 copy-start

commit v3 on v2

--- a/solution.py
+++ b/solution.py
@@ -7,11 +7,10 @@
 
 CHI = 1024
 BLOCK = 128
+BLOCKS = CHI // BLOCK
 TILES = BLOCK // 8
 F32 = jnp.float32
 BF16 = jnp.bfloat16
-
-
 NT = (((1,), (1,)), ((), ()))
 NN = (((1,), (0,)), ((), ()))
 
@@ -20,8 +19,31 @@
     return lax.dot_general(a, b, dims, precision=lax.Precision.HIGHEST, preferred_element_type=F32)
 
 
-def factor_block(r_ref):
+def mul(a, b, dims):
+    return lax.dot_general(a, b, dims, preferred_element_type=F32)
+
+
+def split(x):
+    high = x.astype(BF16)
+    rest = x - high.astype(F32)
+    middle = rest.astype(BF16)
+    return high, middle, (rest - middle.astype(F32)).astype(BF16)
+
+
+def first(x):
+    h, m, l = split(x)
+    return jnp.concatenate([h, h, m, m, h, l], axis=1)
+
+
+def second(x, axis):
+    h, m, l = split(x)
+    return jnp.concatenate([h, m, h, m, l, h], axis=axis)
+
+
+def factor_block(r_ref, shadows):
     sub = lax.broadcasted_iota(jnp.int32, (8, BLOCK), 0)
+    shadows = list(shadows)
+    share = -(-len(shadows) // TILES)
 
     def spread(tile, row):
         return jnp.broadcast_to(tile[row : row + 1, :], (8, BLOCK))
@@ -45,7 +67,6 @@
             lefts.append(ul)
             rights.append(ur)
             links.append(link)
-        r_ref[at, :BLOCK] = left * scale
         r_ref[at, BLOCK:] = right * scale
         for s in range(t + 1, TILES):
             low = pl.ds(8 * s, 8)
@@ -58,48 +79,105 @@
                 left, right = left - below * lefts[i], right - below * rights[i]
             r_ref[low, :BLOCK] = left
             r_ref[low, BLOCK:] = right
-
-
-def factor_kernel(lb_fn, a_ref, g_ref, q_ref, f_ref, r_ref):
-    blocks = CHI // BLOCK
+        for shadow in shadows[t * share : (t + 1) * share]:
+            shadow()
+
+
+def factor_kernel(lb_fn, a_ref, g_ref, q_ref, f_ref, r_ref, c_ref, pa_ref, pb_ref, y_ref, ia_ref, ib_ref):
     row = lax.broadcasted_iota(jnp.int32, (BLOCK, BLOCK), 0)
     col = lax.broadcasted_iota(jnp.int32, (BLOCK, BLOCK), 1)
+    one = jnp.where(row == col, 1.0, 0.0).astype(F32)
+
+    def block(j):
+        return pl.ds(pl.multiple_of(j * BLOCK, BLOCK), BLOCK)
+
+    def chunk(i):
+        return slice(256 * i, 256 * i + 256)
+
+    def keep_inverse():
+        inv = jnp.where(row >= col, r_ref[:, BLOCK:], 0.0)
+        ia_ref[...] = first(inv)
+        ib_ref[...] = second(inv, 1)
+
+    def column(j, i):
+        def run():
+            p = mul(c_ref[chunk(i), :], ib_ref[...], NT)
+            rows = 256 * i + lax.broadcasted_iota(jnp.int32, (256, BLOCK), 0)
+            cols = j * BLOCK + lax.broadcasted_iota(jnp.int32, (256, BLOCK), 1)
+            a_ref[chunk(i), block(j)] = jnp.where(rows >= cols, p, 0.0)
+            h, m, l = split(jnp.where(rows >= (j + 1) * BLOCK, p, 0.0))
+            pa_ref[chunk(i), :] = jnp.concatenate([h, h, m, m, h, l], axis=1)
+            pb_ref[chunk(i), :] = jnp.concatenate([h, m, h, m, l, h], axis=1)
+        return run
+
+    def solve(j, h):
+        def run():
+            y = mul(ia_ref[...], second(g_ref[h, block(j), :], 0), NN)
+            g_ref[h, block(j), :] = y
+            y_ref[h] = second(y, 0)
+        return run
+
+    def ahead(j, i):
+        def run():
+            c = a_ref[chunk(i), block(j + 1)] - mul(pa_ref[chunk(i), :], pb_ref[block(j + 1), :], NT)
+            c_ref[chunk(i), :] = first(c)
+        return run
+
+    def trail(k, i):
+        def run():
+            lo = max(256 * i, BLOCK * k)
+            rows = slice(lo, 256 * i + 256)
+            cols = slice(BLOCK * k, BLOCK * k + BLOCK)
+            a_ref[rows, cols] -= mul(pa_ref[rows, :], pb_ref[cols, :], NT)
+        return run
+
+    def sweep(h, i):
+        def run():
+            at = slice(max(256 * i, BLOCK), 256 * i + 256)
+            g_ref[h, at, :] -= mul(pa_ref[at, :], y_ref[h], NN)
+        return run
+
+    r_ref[:, :BLOCK] = a_ref[:BLOCK, :BLOCK]
+    r_ref[:, BLOCK:] = one
+    factor_block(r_ref, [])
+    keep_inverse()
+    for i in range(4):
+        c_ref[chunk(i), :] = first(a_ref[chunk(i), :BLOCK])
 
     def body(j, carry):
-        here = pl.ds(pl.multiple_of(j * BLOCK, BLOCK), BLOCK)
-        r_ref[:, :BLOCK] = a_ref[here, here]
-        r_ref[:, BLOCK:] = jnp.where(row == col, 1.0, 0.0).astype(F32)
-        factor_block(r_ref)
-        for jj in range(blocks):
-            @pl.when(j == jj)
-            def _():
-                lo, hi = jj * BLOCK, (jj + 1) * BLOCK
-                inv = jnp.where(row >= col, r_ref[:, BLOCK:], 0.0)
-                d = dot(a_ref[lo:hi, lo:hi], inv, NT)
-                a_ref[lo:hi, lo:hi] = jnp.where(row >= col, d, 0.0)
-                y = []
-                for h in range(2):
-                    yh = dot(inv, g_ref[h, lo:hi, :], NN)
-                    g_ref[h, lo:hi, :] = yh
-                    y.append(yh)
-                if hi < CHI:
-                    a_ref[hi:, lo:hi] = dot(a_ref[hi:, lo:hi], inv, NT)
-                for i in range(jj + 1, blocks):
-                    mine = pl.ds(i * BLOCK, BLOCK)
-                    p = a_ref[mine, lo:hi]
-                    a_ref[mine, hi : (i + 1) * BLOCK] -= dot(p, a_ref[hi : (i + 1) * BLOCK, lo:hi], NT)
-                    for h in range(2):
-                        g_ref[h, mine, :] -= dot(p, y[h], NN)
+        p = mul(c_ref[block(j + 1), :], ib_ref[...], NT)
+        r_ref[:, :BLOCK] = a_ref[block(j + 1), block(j + 1)] - mul(first(p), second(p, 1), NT)
+        r_ref[:, BLOCK:] = one
+        shadows = [column(j, i) for i in range(4)] + [solve(j, h) for h in range(2)] + [ahead(j, i) for i in range(4)]
+        shadows += [trail(k, i) for k in range(2, BLOCKS) for i in range(k // 2, 4)]
+        shadows += [sweep(h, i) for h in range(2) for i in range(4)]
+        factor_block(r_ref, shadows)
+        keep_inverse()
         return carry
 
-    lax.fori_loop(0, blocks, body, 0)
+    lax.fori_loop(0, BLOCKS - 1, body, 0)
+    for i in range(4):
+        column(BLOCKS - 1, i)()
+    for h in range(2):
+        solve(BLOCKS - 1, h)()
     lb = lb_fn()
     at = pl.ds(pl.multiple_of(lb * 64, 64), 64)
     for h in range(2):
         q_ref[h] = g_ref[h, at, :] * 128.0
-    rr = lb * 64 + lax.broadcasted_iota(jnp.int32, (64, CHI), 0)
-    cc = lax.broadcasted_iota(jnp.int32, (64, CHI), 1)
-    f_ref[...] = jnp.where(rr >= cc, a_ref[at, :], 0.0) * (1.0 / 128.0)
+    f_ref[...] = a_ref[at, :] * (1.0 / 128.0)
+
+
+SCRATCH = [
+    pltpu.VMEM((CHI, CHI), F32),
+    pltpu.VMEM((2, CHI, BLOCK), F32),
+    pltpu.VMEM((BLOCK, 2 * BLOCK), F32),
+    pltpu.VMEM((CHI, 6 * BLOCK), BF16),
+    pltpu.VMEM((CHI, 6 * BLOCK), BF16),
+    pltpu.VMEM((CHI, 6 * BLOCK), BF16),
+    pltpu.VMEM((2, 6 * BLOCK, BLOCK), BF16),
+    pltpu.VMEM((BLOCK, 6 * BLOCK), BF16),
+    pltpu.VMEM((BLOCK, 6 * BLOCK), BF16),
+]
 
 
 MESH = pl.DeviceIdType.MESH
@@ -134,79 +212,106 @@
     def far_first(n):
         return sorted(range(1, n), key=lambda d: -min(d, n - d))
 
-    copies = []
-    for d in far_first(ny):
-        to = mod(y + d, ny)
-        copy = remote(part_ref.at[pl.ds(2 * to, 2)], a_recv.at[d - 1], a_send.at[d - 1], a_got.at[d - 1], {"rep": to})
-        copy.start()
-        copies.append(copy)
-    mine = part_ref[pl.ds(2 * y, 2)]
-    for copy, d in sorted(zip(copies, far_first(ny)), key=lambda pair: min(pair[1], ny - pair[1])):
-        copy.wait_recv()
-        mine = mine + a_recv[d - 1]
     rows = pl.ds(pl.multiple_of(lb * 64, 64), 64)
+    sent = []
+
+    arriving = {}
     for e in range(2):
-        grown_ref[e, rows, :] = mine[e]
-    sent = list(copies)
+        for d in far_first(ny):
+            to = mod(y + d, ny)
+            at = e * (ny - 1) + d - 1
+            copy = remote(part_ref.at[2 * to + e], a_recv.at[at], a_send.at[at], a_got.at[at], {"rep": to})
+            copy.start()
+            arriving[e, d] = copy
+            sent.append(copy)
+
+    def near_first(n):
+        return sorted(range(1, n), key=lambda d: min(d, n - d))
+
+    def settle(e):
+        mine = part_ref[2 * y + e]
+        for d in near_first(ny):
+            arriving[e, d].wait_recv()
+            mine = mine + a_recv[e * (ny - 1) + d - 1]
+        grown_ref[e, rows, :] = mine
 
     def block(e, chip, which):
         return grown_ref.at[e, pl.ds(pl.multiple_of((2 * chip + which) * 64, 64), 64)]
 
     partner = {"lb": 2 * x + 1 - core}
-    handed = []
-
-    def hand(e, chip, slot):
+    handed = {}
+
+    def hand(e, step, direction):
+        chip = mod(x - direction * step, nx)
+        slot = ((0 if direction > 0 else 1) * (half + 1) + step) * 2 + e
         copy = remote(block(e, chip, core), block(e, chip, core), p_send.at[slot], p_got.at[slot], partner)
         copy.start()
-        handed.append(copy)
+        handed[direction, step, e] = copy
+        sent.append(copy)
+
+    flying = {}
 
     def ring(direction, step, e):
         chip = mod(x - direction * (step - 1), nx)
-        side = 0 if direction > 0 else 1
-        slot = (side * half + step - 1) * 2 + e
+        slot = ((0 if direction > 0 else 1) * half + step - 1) * 2 + e
         to = {"lb": 2 * mod(x + direction, nx) + core}
         copy = remote(block(e, chip, core), block(e, chip, core), b_send.at[slot], b_got.at[slot], to)
         copy.start()
+        flying[direction, step, e] = copy
         sent.append(copy)
-        return copy
-
-    def moves(step):
-        full = [(direction, e) for e in range(2) for direction in (1, -1)]
-        return full if step < half else [(1, 0), (-1, 1)]
-
-    flying = {}
-    for direction, e in moves(1):
-        flying[direction, 1, e] = ring(direction, 1, e)
+
+    def ways(step, e):
+        return (1, -1) if step < half else ((1,) if e == 0 else (-1,))
+
+    def launch(e):
+        for direction in ways(1, e):
+            ring(direction, 1, e)
+        hand(e, 0, 1)
+
+    def advance(step, e):
+        for direction in ways(step, e):
+            flying[direction, step, e].wait_recv()
+            if step < half and direction in ways(step + 1, e):
+                ring(direction, step + 1, e)
+            hand(e, step, direction)
+
+    def product(chip):
+        at = pl.ds(pl.multiple_of(chip * 128, 128), 128)
+        ours = [grown_ref[e, rows, :] for e in range(2)]
+        products[chip] = dot(ours[0], grown_ref[0, at, :], NT) + dot(ours[1], grown_ref[1, at, :], NT)
+
+        @pl.when(chip != z)
+        def _():
+            remote(products.at[chip], z_recv.at[z], c_send.at[chip], c_got.at[z], {"rb": chip}).start()
+
+    settle(0)
+    launch(0)
+    advance(1, 0)
+    settle(1)
+    launch(1)
     for e in range(2):
-        hand(e, x, e)
-    slot = 2
+        handed[1, 0, e].wait_recv()
+    product(x)
     for step in range(1, half + 1):
-        for direction, e in moves(step):
-            flying[direction, step, e].wait_recv()
-            if step < half and (direction, e) in moves(step + 1):
-                flying[direction, step + 1, e] = ring(direction, step + 1, e)
-            hand(e, mod(x - direction * step, nx), slot)
-            slot += 1
-    for copy in handed:
+        if step > 1:
+            advance(step, 0)
+        advance(step, 1)
+        if step < half:
+            for direction in (1, -1):
+                for e in range(2):
+                    handed[direction, step, e].wait_recv()
+                product(mod(x - direction * step, nx))
+    handed[1, half, 0].wait_recv()
+    handed[-1, half, 1].wait_recv()
+    product(mod(x + half, nx))
+    summed = products[z]
+    for d in near_first(nz):
+        far = mod(z + d, nz)
+        copy = remote(products.at[far], z_recv.at[far], c_send.at[far], c_got.at[far], {"rb": far})
         copy.wait_recv()
-    sent += handed
-
-    ours = [grown_ref[e, rows, :] for e in range(2)]
-    copies = []
-    for d in far_first(nz) + [0]:
-        to = mod(z + d, nz)
-        at = pl.ds(pl.multiple_of(to * 128, 128), 128)
-        products[d] = dot(ours[0], grown_ref[0, at, :], NT) + dot(ours[1], grown_ref[1, at, :], NT)
-        if d:
-            copy = remote(products.at[d], z_recv.at[d - 1], c_send.at[d - 1], c_got.at[d - 1], {"rb": to})
-            copy.start()
-            copies.append((d, copy))
-    summed = products[0]
-    for d, copy in sorted(copies, key=lambda pair: min(pair[0], nz - pair[0])):
-        copy.wait_recv()
-        summed = summed + z_recv[d - 1]
+        summed = summed + z_recv[far]
+        sent.append(copy)
     total[...] = summed
-    sent += [copy for _, copy in copies]
     copies = []
     for d in far_first(ny):
         to = mod(y + d, ny)
@@ -252,16 +357,17 @@
         pltpu.make_async_copy(tile, landed, e_got.at[i]).wait()
 
     n = ny
-    copies = []
     chunk = gram_ref.at[core, outer, inner]
     for d in far_first(n):
         to = {"rep": mod(y + d * (1 - core), n), "rb": mod(z + d * core, n)}
-        copy = remote(chunk, chunk, f_send.at[d - 1], f_got.at[d - 1], to)
-        copy.start()
-        copies.append(copy)
-    for copy in copies:
-        copy.wait_recv()
-    sent += copies
+        copy = remote(chunk, chunk, f_send.at[d], f_got.at[inner], to)
+        copy.start()
+        sent.append(copy)
+
+    def gathered(position):
+        @pl.when(position != inner)
+        def _():
+            remote(chunk, chunk, f_send.at[0], f_got.at[position], partner).wait_recv()
 
     cuts = 4
     width = n // cuts
@@ -292,9 +398,11 @@
         return [(1 if cut < cuts // 2 else -1, cut) for cut in (0, cuts // 2, 1, cuts // 2 + 1)]
 
     flying = {}
-    for direction, cut in turns(1):
-        flying[direction, 1, cut] = around(direction, 1, cut)
     for cut in range(cuts):
+        for position in range(cut * width, cut * width + width):
+            gathered(position)
+        for direction in (1, -1):
+            flying[direction, 1, cut] = around(direction, 1, cut)
         share(outer, cut, cut)
     slot = cuts
     for step in range(1, middle + 1):
@@ -313,7 +421,7 @@
 def gather_call(part, sizes):
     nx, nz, ny = sizes
     vm = pl.BlockSpec(memory_space=pltpu.VMEM)
-    counts = [ny - 1] * 2 + [2 * nx] * 4 + [nz - 1] * 2 + [ny - 1] * 2 + [nx] * 2 + [ny - 1] * 2 + [4 * ny] * 4
+    counts = [2 * (ny - 1)] * 2 + [2 * nx] * 2 + [2 * nx + 4] * 2 + [nz] * 2 + [ny - 1] * 2 + [nx] * 2 + [ny] * 2 + [4 * ny] * 4
 
     def kernel(part_ref, grown_ref, gram_ref, a_recv, products, z_recv, total, y_recv, tile, *sems):
         gather_kernel(sizes, part_ref, grown_ref, gram_ref, a_recv, products, z_recv, total, y_recv, tile, sems)
@@ -327,9 +435,9 @@
         in_specs=[vm],
         out_specs=(vm, vm),
         scratch_shapes=[
-            pltpu.VMEM((ny - 1, 2, 64, 128), F32),
+            pltpu.VMEM((2 * (ny - 1), 64, 128), F32),
             pltpu.VMEM((nz, 64, 128), F32),
-            pltpu.VMEM((nz - 1, 64, 128), F32),
+            pltpu.VMEM((nz, 64, 128), F32),
             pltpu.VMEM((64, 128), F32),
             pltpu.VMEM((ny - 1, 8, 128), F32),
             pltpu.VMEM((8, 128), F32),
@@ -340,7 +448,7 @@
 
 
 def factor_call(gram, grown, lb_fn):
-    def kernel(a_in, g_in, q_ref, f_ref, a_ref, g_ref, r_ref):
+    def kernel(a_in, g_in, q_ref, f_ref, a_ref, g_ref, *scratch):
         for outer in range(8):
             for inner in range(8):
                 for i in range(8):
@@ -349,7 +457,7 @@
                     a_ref[up : up + 8, 128 * outer : 128 * outer + 128] = a_in[0, outer, inner, at, :]
                     a_ref[low : low + 8, 128 * inner : 128 * inner + 128] = a_in[1, outer, inner, at, :]
         g_ref[...] = g_in[...]
-        factor_kernel(lb_fn, a_ref, g_ref, q_ref, f_ref, r_ref)
+        factor_kernel(lb_fn, a_ref, g_ref, q_ref, f_ref, *scratch)
 
     vm = pl.BlockSpec(memory_space=pltpu.VMEM)
     return pl.pallas_call(
@@ -357,7 +465,7 @@
         out_shape=(jax.ShapeDtypeStruct((2, 64, 128), F32), jax.ShapeDtypeStruct((64, CHI), F32)),
         in_specs=[vm, vm],
         out_specs=(vm, vm),
-        scratch_shapes=[pltpu.VMEM((CHI, CHI), F32), pltpu.VMEM((2, CHI, 128), F32), pltpu.VMEM((BLOCK, 2 * BLOCK), F32)],
+        scratch_shapes=SCRATCH,
         compiler_params=pltpu.CompilerParams(vmem_limit_bytes=24 << 20),
     )(gram, grown)
 

time: 147 us -> 135 us (0.918)
  Pallas kernels: 143 us -> 130 us
    pallas_call x1, Pallas kernels: 49 us -> 42.1 us  [factor_call(): pl.pallas_call(kernel, out_shape=(jax.ShapeDtypeStruct((2, 64, 128), F32)...]
    pallas_call x1, Pallas kernels: 93.7 us -> 88.3 us  [gather_call(): pl.pallas_call(kernel, out_shape=(jax.ShapeDtypeStruct((2, 128 * nx, 128)...]
where the time goes in v3:
time: 135 us; the launch traced here: 134 us
  Pallas kernels  130 us (96%)
  matrix products  2.25 us (2%)
    pallas_call x1, Pallas kernels, gather_call(): pl.pallas_call(kernel, out_shape=(jax.ShapeDtypeStruct((2, 128 * nx, 128)...  88.3 us
    pallas_call x1, Pallas kernels, factor_call(): pl.pallas_call(kernel, out_shape=(jax.ShapeDtypeStruct((2, 64, 128), F32)...  42.1 us

profile of v3, /device:TPU:1, one launch (start us, length us, event | category | flops | bytes accessed | tf_op | source)
XLA Modules:
  0.0 134.4 jit_solution(8512956443148261345)
XLA Ops:
  0.6 0.0 copy-start
  0.6 1.0 copy-done
  1.7 1.3 fusion.3
  3.0 0.9 convolution_bitcast_fusion.part_ref
  3.9 88.3 %shard_map.50 = (f32[2,1024,128]{2,1,0:T(8,128)S(1)}, f32[2,8,8,64,128]{4,3,2,1,0:T(8,128)S(1)}) custom-call(f32[16,64,128]{2,1,0:T(8,128)S(1)} %convolution_bitcast_fusion.part_ref), custom_call_target="tpu_custom_call" | custom-call | tf_op jit(solution)/shard_map/pallas_call | solution.py:429
  92.3 42.1 %shard_map.51 = (f32[2,64,128]{2,1,0:T(8,128)}, f32[64,1024]{1,0:T(8,128)}) custom-call(f32[2,8,8,64,128]{4,3,2,1,0:T(8,128)S(1)} %get-tuple-element.4.a_in, f32[2,1024,128]{2,1,0:T(8,128)S(1)} %get-tuple-element.5.g_in), custom_call_target="tpu_custom_call" | custom-call | tf_op jit(solution)/shard_map/pallas_call | solution.py:463
Async XLA Ops:
  0.6 1.0 copy-start

commit v4 on v3

--- a/solution.py
+++ b/solution.py
@@ -48,18 +48,25 @@
     def spread(tile, row):
         return jnp.broadcast_to(tile[row : row + 1, :], (8, BLOCK))
 
+    def lane(tile, at):
+        return jnp.broadcast_to(tile[:, at : at + 1], (8, BLOCK))
+
+    coming = []
     for t in range(TILES):
         at = pl.ds(8 * t, 8)
         left, right = r_ref[at, :BLOCK], r_ref[at, BLOCK:]
-        cols = [jnp.broadcast_to(left[:, 8 * t + n : 8 * t + n + 1], (8, BLOCK)) for n in range(8)]
+        cols = coming if t else [lane(left, n) for n in range(8)]
         roots, lefts, rights, links = [], [], [], []
         scale = jnp.zeros((8, BLOCK), F32)
+        pivot = spread(cols[0], 0)
         for i in range(8):
-            root = lax.rsqrt(spread(cols[i], i))
+            root = lax.rsqrt(pivot)
             scale = jnp.where(sub == i, root, scale)
-            below = jnp.where(sub > i, cols[i] * root, 0.0)
+            below = jnp.where(sub > i, cols[i], 0.0) * root
             ul, ur = spread(left, i) * root, spread(right, i) * root
             link = {n: spread(cols[n], i) * root for n in range(i + 1, 8)}
+            if i < 7:
+                pivot = spread(cols[i + 1], i + 1) - link[i + 1] * link[i + 1]
             for n in range(i + 1, 8):
                 cols[n] = cols[n] - below * link[n]
             left, right = left - below * ul, right - below * ur
@@ -71,9 +78,13 @@
         for s in range(t + 1, TILES):
             low = pl.ds(8 * s, 8)
             left, right = r_ref[low, :BLOCK], r_ref[low, BLOCK:]
-            cols = [jnp.broadcast_to(left[:, 8 * t + n : 8 * t + n + 1], (8, BLOCK)) for n in range(8)]
+            cols = [lane(left, 8 * t + n) for n in range(8)]
+            if s == t + 1:
+                coming = [lane(left, 8 * s + n) for n in range(8)]
             for i in range(8):
                 below = cols[i] * roots[i]
+                if s == t + 1:
+                    coming = [coming[n] - below * spread(below, n) for n in range(8)]
                 for n in range(i + 1, 8):
                     cols[n] = cols[n] - below * links[i][n]
                 left, right = left - below * lefts[i], right - below * rights[i]
@@ -187,7 +198,7 @@
     return lax.rem(value + 2 * size, size)
 
 
-def gather_kernel(sizes, part_ref, grown_ref, gram_ref, a_recv, products, z_recv, total, y_recv, tile, sems):
+def gather_kernel(sizes, part_ref, grown_ref, gram_ref, a_recv, joined, products, z_recv, total, y_recv, tile, sems):
     nx, nz, ny = sizes
     lb, z, y = lax.axis_index("lb"), lax.axis_index("rb"), lax.axis_index("rep")
     x, core = lb // 2, lax.rem(lb, 2)
@@ -215,22 +226,40 @@
     rows = pl.ds(pl.multiple_of(lb * 64, 64), 64)
     sent = []
 
-    arriving = {}
-    for e in range(2):
-        for d in far_first(ny):
-            to = mod(y + d, ny)
-            at = e * (ny - 1) + d - 1
-            copy = remote(part_ref.at[2 * to + e], a_recv.at[at], a_send.at[at], a_got.at[at], {"rep": to})
-            copy.start()
-            arriving[e, d] = copy
-            sent.append(copy)
-
     def near_first(n):
         return sorted(range(1, n), key=lambda d: min(d, n - d))
 
+    opposite = ny // 2
+    arriving = {}
+
+    def deliver(e, d, src):
+        at = e * (ny - 1) + d - 1
+        copy = remote(src, a_recv.at[at], a_send.at[at], a_got.at[at], {"rep": mod(y + d, ny)})
+        copy.start()
+        arriving[e, d] = copy
+        sent.append(copy)
+
+    handing = []
+    for e, turn in ((0, 1), (1, -1)):
+        src = part_ref.at[2 * mod(y + opposite, ny) + e]
+        at = e * (ny - 1) + opposite - 1
+        copy = remote(src, a_recv.at[at], a_send.at[at], a_got.at[at], {"rep": mod(y + turn, ny)})
+        copy.start()
+        handing.append(copy)
+        sent.append(copy)
+    for e, turn in ((0, 1), (1, -1)):
+        late = (opposite - turn) % ny
+        for d in far_first(ny):
+            if d not in (opposite, late):
+                deliver(e, d, part_ref.at[2 * mod(y + d, ny) + e])
+        handing[e].wait_recv()
+        joined[e] = a_recv[e * (ny - 1) + opposite - 1] + part_ref[2 * mod(y + late, ny) + e]
+        deliver(e, late, joined.at[e])
+
     def settle(e):
         mine = part_ref[2 * y + e]
-        for d in near_first(ny):
+        late = opposite - 1 if e == 0 else opposite + 1
+        for d in [d for d in near_first(ny) if d not in (opposite, late)] + [late]:
             arriving[e, d].wait_recv()
             mine = mine + a_recv[e * (ny - 1) + d - 1]
         grown_ref[e, rows, :] = mine
@@ -423,8 +452,8 @@
     vm = pl.BlockSpec(memory_space=pltpu.VMEM)
     counts = [2 * (ny - 1)] * 2 + [2 * nx] * 2 + [2 * nx + 4] * 2 + [nz] * 2 + [ny - 1] * 2 + [nx] * 2 + [ny] * 2 + [4 * ny] * 4
 
-    def kernel(part_ref, grown_ref, gram_ref, a_recv, products, z_recv, total, y_recv, tile, *sems):
-        gather_kernel(sizes, part_ref, grown_ref, gram_ref, a_recv, products, z_recv, total, y_recv, tile, sems)
+    def kernel(part_ref, grown_ref, gram_ref, a_recv, joined, products, z_recv, total, y_recv, tile, *sems):
+        gather_kernel(sizes, part_ref, grown_ref, gram_ref, a_recv, joined, products, z_recv, total, y_recv, tile, sems)
 
     return pl.pallas_call(
         kernel,
@@ -436,6 +465,7 @@
         out_specs=(vm, vm),
         scratch_shapes=[
             pltpu.VMEM((2 * (ny - 1), 64, 128), F32),
+            pltpu.VMEM((2, 64, 128), F32),
             pltpu.VMEM((nz, 64, 128), F32),
             pltpu.VMEM((nz, 64, 128), F32),
             pltpu.VMEM((64, 128), F32),

time: 135 us -> 128 us (0.948)
  Pallas kernels: 130 us -> 123 us
    pallas_call x1, Pallas kernels: 42.1 us -> 35.7 us  [factor_call(): pl.pallas_call(kernel, out_shape=(jax.ShapeDtypeStruct((2, 64, 128), F32)...]
where the time goes in v4:
time: 128 us; the launch traced here: 127 us
  Pallas kernels  123 us (96%)
  matrix products  2.25 us (2%)
    pallas_call x1, Pallas kernels, gather_call(): pl.pallas_call(kernel, out_shape=(jax.ShapeDtypeStruct((2, 128 * nx, 128)...  87.8 us
    pallas_call x1, Pallas kernels, factor_call(): pl.pallas_call(kernel, out_shape=(jax.ShapeDtypeStruct((2, 64, 128), F32)...  35.7 us

profile of v4, /device:TPU:1, one launch (start us, length us, event | category | flops | bytes accessed | tf_op | source)
XLA Modules:
  0.0 127.4 jit_solution(2939593987565773663)
XLA Ops:
  0.6 0.0 copy-start
  0.6 1.0 copy-done
  1.7 1.3 %fusion.3 = bf16[16,128,128]{2,0,1:T(8,128)(2,1)S(1)} fusion(bf16[128,16,128]{2,1,0:T(8,128)(2,1)S(1)} %copy-done, f32[16,16]{1,0:T(8,128)} %param.5), kind=kOutput, calls=%fused_computation.4 | convolution fusion | flops 50331648 | bytes 1049600 | tf_op jit(solution)/shard_map/kur,ue->ker/dot_general | solution.py:505
  3.0 0.9 convolution_bitcast_fusion.part_ref
  3.9 87.8 %shard_map.50 = (f32[2,1024,128]{2,1,0:T(8,128)S(1)}, f32[2,8,8,64,128]{4,3,2,1,0:T(8,128)S(1)}) custom-call(f32[16,64,128]{2,1,0:T(8,128)S(1)} %convolution_bitcast_fusion.part_ref), custom_call_target="tpu_custom_call" | custom-call | tf_op jit(solution)/shard_map/pallas_call | solution.py:458
  91.7 35.7 %shard_map.51 = (f32[2,64,128]{2,1,0:T(8,128)}, f32[64,1024]{1,0:T(8,128)}) custom-call(f32[2,8,8,64,128]{4,3,2,1,0:T(8,128)S(1)} %get-tuple-element.4.a_in, f32[2,1024,128]{2,1,0:T(8,128)S(1)} %get-tuple-element.5.g_in), custom_call_target="tpu_custom_call" | custom-call | tf_op jit(solution)/shard_map/pallas_call | solution.py:493
Async XLA Ops:
  0.6 1.0 copy-start
